TPU v7x, 32 devices: a whole 2x2x4 slice. The times are simulated.
32 devices in a mesh: seg: 8 (over z, x), rep: 4 (over y, core).
Axes of the slice: x: 2, y: 2, z: 4, core: 2. Of those that a mesh axis runs over, the one named last changes fastest.
Arguments:
- decoder_rows: bfloat16 [256, 4096], P('rep', 'seg'), may hold values from -2000 to 2000
- norm_gain: float32 [4096], replicated, may hold values from 0.5 to 1.5
- query_weight: bfloat16 [4096, 4096], P('rep', 'seg'), may hold values from -1 to 1
- key_codes: bfloat16 [4, 4096, 4096], P('rep', 'seg'), may hold values from -127 to 127, as said below
- key_scale: float32 [4, 32, 64], P('rep', 'seg'), may hold values from 0.5 to 1.5
- value_codes: bfloat16 [4, 4096, 4096], P('rep', 'seg'), may hold values from -6 to 6
- value_scale: float32 [4, 32, 64], P('rep', 'seg'), may hold values from 0.5 to 2
- enc_lengths: int32 [4], P('rep'), may hold values from 1024 to 4096
- output_weight: bfloat16 [4096, 4096], P('seg', 'rep'), may hold values from -0.09375 to 0.09375
Outputs:
- update: bfloat16 [256, 4096], P('rep', 'seg')
Inputs may be any that keep to these rules, and one draw needn't show every extreme that they name: `key_codes`: codes of a block times its scale give the cached keys.
All inputs are finite; a program needn't handle non-finite values.
Results may differ from a plain program's by a relative error of at most 0.011.
Values may be sent and summed in bfloat16 or wider, within the bound.
A program may use at most 64 MiB of HBM per device.

v0:
```python
import jax
import jax.numpy as jnp
from jax import lax
from jax.sharding import PartitionSpec as P


def per_device(
    decoder_rows,
    norm_gain,
    query_weight,
    key_codes,
    key_scale,
    value_codes,
    value_scale,
    enc_lengths,
    output_weight,
):
    gathered = lax.all_gather(decoder_rows, "seg", axis=1, tiled=True)
    widened = gathered.astype(jnp.float32)
    variance = jnp.mean(widened * widened, axis=-1, keepdims=True)
    normed = (widened * lax.rsqrt(variance + 1e-06) * norm_gain[None, :]).astype(jnp.bfloat16)
    query_own = jnp.dot(
        normed,
        lax.all_gather(query_weight, "rep", axis=0, tiled=True),
        preferred_element_type=jnp.float32,
    ).astype(jnp.bfloat16)
    queries = lax.all_gather(query_own, "seg", axis=1, tiled=True)
    docs_here, seg_length, inner_width = key_codes.shape
    head_count = key_scale.shape[2]
    head_dim = inner_width // head_count
    block_length = seg_length // key_scale.shape[1]
    per_doc = queries.shape[0] // docs_here
    row_count = docs_here * per_doc
    first_pos = lax.axis_index("seg") * seg_length
    positions = first_pos + jnp.arange(seg_length, dtype=jnp.int32)

    def one_doc(group_members):
        (
            document_query,
            document_keys,
            document_values,
            document_key_scale,
            document_value_scale,
            document_length,
        ) = group_members
        split_query = document_query.reshape(per_doc, head_count, head_dim)
        split_keys = document_keys.reshape(seg_length, head_count, head_dim)
        split_values = document_values.reshape(seg_length, head_count, head_dim)
        attention_scores = jnp.einsum(
            "qhd,khd->qhk", split_query, split_keys, preferred_element_type=jnp.float32
        )
        key_multiplier = jnp.repeat(document_key_scale, block_length, axis=0).T
        value_factor = jnp.repeat(document_value_scale, block_length, axis=0).T
        attention_scores = attention_scores * key_multiplier[None]
        usable = (positions < document_length)[None, None, :]
        attention_scores = jnp.where(usable, attention_scores, jnp.float32(-1e30))
        peaks = jnp.max(attention_scores, axis=-1)
        weights = jnp.where(usable, jnp.exp(attention_scores - peaks[..., None]), jnp.float32(0.0))
        totals = jnp.sum(weights, axis=-1)
        scaled = (weights * value_factor[None]).astype(jnp.bfloat16)
        attended = jnp.einsum(
            "qhk,khd->qhd", scaled, split_values, preferred_element_type=jnp.float32
        )
        return (peaks, totals, attended.reshape(per_doc, inner_width))

    query_docs = queries.reshape(docs_here, per_doc, inner_width)
    peaks, totals, outputs = lax.map(
        one_doc, (query_docs, key_codes, value_codes, key_scale, value_scale, enc_lengths)
    )
    peaks = peaks.reshape(row_count, head_count)
    totals = totals.reshape(row_count, head_count)
    outputs = outputs.reshape(row_count, inner_width)
    seg_count = lax.axis_size("seg")
    own_heads = head_count // seg_count
    received = (
        lax.all_to_all(peaks[None], "seg", split_axis=2, concat_axis=0, tiled=True),
        lax.all_to_all(totals[None], "seg", split_axis=2, concat_axis=0, tiled=True),
        lax.all_to_all(outputs[None], "seg", split_axis=2, concat_axis=0, tiled=True),
    )
    peak_all, total_all, out_all = received
    largest = jnp.max(peak_all, axis=0)
    factor = jnp.exp(peak_all - largest[None])
    denominator = jnp.sum(factor * total_all, axis=0)
    numerator = jnp.sum(
        out_all.reshape(seg_count, row_count, own_heads, head_dim) * factor[..., None], axis=0
    )
    attn_own = (
        (numerator / denominator[..., None])
        .reshape(row_count, own_heads * head_dim)
        .astype(jnp.bfloat16)
    )
    partial_terms = jnp.dot(
        attn_own,
        lax.all_gather(output_weight, "rep", axis=1, tiled=True),
        preferred_element_type=jnp.float32,
    )
    return lax.psum_scatter(partial_terms, "seg", scatter_dimension=1, tiled=True).astype(
        jnp.bfloat16
    )


def solution(mesh):
    placed = (
        P("rep", "seg"),
        P(),
        P("rep", "seg"),
        P("rep", "seg", None),
        P("rep", "seg", None),
        P("rep", "seg", None),
        P("rep", "seg", None),
        P("rep"),
        P("seg", "rep"),
    )
    return jax.shard_map(
        per_device, mesh=mesh, in_specs=placed, out_specs=P("rep", "seg"), check_vma=False
    )
```

profile of v0, /device:TPU:0, one launch (start us, length us, event | category | flops | bytes accessed | tf_op | source)
XLA Modules:
  0.0 250.8 jit_solution(3098906229739473497)
XLA Ops:
  6.5 0.7 all-gather.3.cloned.1.call-update
  7.3 0.7 all-gather.5.cloned.1.call-update
  8.0 0.8 copy.36
  9.6 6.6 %copy.34 = bf16[1,512,4096]{1,2,0:T(8,128)(2,1)} copy(bf16[1,512,4096]{2,1,0:T(8,128)(2,1)} %param.12) | data formatting | bytes 8388608 | tf_op args[3]
  16.2 33.2 %all_gather.12 = bf16[64,4096]{1,0:T(8,128)(2,1)S(1)} all-gather(bf16[64,512]{1,0:T(8,128)(2,1)S(1)} %copy-done.1), channel_id=1, replica_groups=mesh['seg'=8,'rep'=4] {'seg'}, dimensions={1}, use_global_device_ids=true | all-gather | bytes 589824 | tf_op jit(solution)/shard_map/all_gather | solution.py:18
  49.6 3.1 %convolution_convert_fusion = bf16[64,512]{1,0:T(8,128)(2,1)S(1)} fusion(bf16[4096,512]{1,0:T(8,128)(2,1)} %all-gather.3.cloned.1.call-done, bf16[64,4096]{1,0:T(8,128)(2,1)S(1)} %all_gather.12, f32[4096]{0:T(1024)S(1)} %copy-done.2, f32[64]{0:T(128)S(1)} %add_rsqrt_fusion), kind=kOutput, calls=%fused_computation.20 | convolution fusion | flops 269516800 | bytes 4800768 | tf_op jit(solution)/shard_map/dot_general | solution.py:22
  52.7 31.6 %all_gather.14 = bf16[64,4096]{1,0:T(8,128)(2,1)S(1)} all-gather(bf16[64,512]{1,0:T(8,128)(2,1)S(1)} %convolution_convert_fusion), channel_id=1, replica_groups=mesh['seg'=8,'rep'=4] {'seg'}, dimensions={1}, use_global_device_ids=true | all-gather | bytes 589824 | tf_op jit(solution)/shard_map/all_gather | solution.py:27
  84.3 1.1 reshape.64
  85.4 4.2 %bitcast_reduce_fusion = (f32[64,64]{0,1:T(8,128)S(1)}, f32[64,64,512]{2,1,0:T(8,128)S(1)}) fusion(f32[64,512]{1,0:T(8,128)S(1)} %bitcast.79, pred[512]{0:T(512)(128)(4,1)S(1)} %add_compare_fusion, bf16[512,64,64]{0,2,1:T(8,128)(2,1)} %bitcast.75, bf16[64,64,64]{2,1,0:T(8,128)(2,1)S(1)} %reshape.64), kind=kOutput, calls=%fused_computation.1 | convolution fusion | flops 274722816 | bytes 13255168 | tf_op jit(solution)/shard_map/while/body/eval_jaxpr/qhd,khd->qhk/dot_general | solution.py:49
  89.6 2.8 %fusion.2 = f32[64,64]{0,1:T(8,128)S(1)} fusion(f32[64,64,512]{2,1,0:T(8,128)S(1)} %get-tuple-element.28, f32[64,64]{0,1:T(8,128)S(1)} %get-tuple-element.27, f32[64,512]{1,0:T(8,128)S(1)} %bitcast.80, pred[512]{0:T(512)(128)(4,1)S(1)} %add_compare_fusion), kind=kLoop, calls=%fused_computation.6 | loop fusion | flops 10481664 | bytes 8552960 | tf_op jit(solution)/shard_map/while/body/eval_jaxpr/reduce_sum | solution.py:59
  92.4 0.4 copy-done
  92.8 0.5 broadcast.37
  93.3 0.7 reduce.4
  94.0 0.7 reshape.73
  94.7 5.3 %all-to-all-start.2 = ((f32[8,1,512]{2,1,0:T(1,128)}), f32[8,1,512]{2,1,0:T(1,128)S(1)}, u32[]{:S(2)}, u32[]{:S(2)}) async-start(f32[8,1,512]{2,1,0:T(1,128)} %reshape.73), calls=%async_computation.2 | async-start | bytes 32768 | tf_op jit(solution)/shard_map/all_to_all | solution.py:77
  100.1 6.5 %copy.39 = bf16[1,512,4096]{1,2,0:T(8,128)(2,1)} copy(bf16[1,512,4096]{2,1,0:T(8,128)(2,1)} %param.14) | data formatting | bytes 8388608 | tf_op args[5]
  106.8 0.7 reduce.6
  107.5 0.7 reshape.71
  108.2 6.0 %all-to-all-start.1 = ((f32[8,1,512]{2,1,0:T(1,128)}), f32[8,1,512]{2,1,0:T(1,128)S(1)}, u32[]{:S(2)}, u32[]{:S(2)}) async-start(f32[8,1,512]{2,1,0:T(1,128)} %reshape.71), calls=%async_computation.1 | async-start | bytes 32768 | tf_op jit(solution)/shard_map/all_to_all | solution.py:76
  114.2 8.5 %fusion.12 = f32[64,64,64]{2,0,1:T(8,128)} fusion(bf16[512,64,64]{0,2,1:T(8,128)(2,1)} %bitcast.78, f32[64,64,512]{2,1,0:T(8,128)} %copy-done, f32[64,512]{1,0:T(8,128)S(1)} %bitcast.88, f32[64,64]{0,1:T(8,128)S(1)} %get-tuple-element.27, f32[64,512]{1,0:T(8,128)S(1)} %bitcast.81, pred[512]{0:T(512)(128)(4,1)S(1)} %add_compare_fusion), kind=kOutput, calls=%fused_computation.17 | convolution fusion | flops 281018368 | bytes 13910528 | tf_op jit(solution)/shard_map/while/body/eval_jaxpr/qhk,khd->qhd/dot_general | solution.py:61
  122.7 1.9 copy.42
  124.6 19.3 %reduce.2 = f32[4096,64]{1,0:T(8,128)} reduce(f32[4096,1,64]{2,1,0:T(1,128)S(1)} %bitcast.77, f32[]{:T(128)} %broadcast.37), dimensions={1}, to_apply=%bitcast.59.reduce_sub_computation | reduce | bytes 2097156
  144.0 3.4 %reshape.69 = f32[8,1,32768]{2,1,0:T(1,128)} reshape(f32[4096,64]{1,0:T(8,128)} %reduce.2) | data formatting | bytes 2097152
  147.3 6.0 %all-to-all-start = ((f32[8,1,32768]{2,1,0:T(1,128)}), f32[8,1,32768]{2,1,0:T(1,128)S(1)}, u32[]{:S(2)}, u32[]{:S(2)}) async-start(f32[8,1,32768]{2,1,0:T(1,128)} %reshape.69), calls=%async_computation | async-start | bytes 2097152 | tf_op jit(solution)/shard_map/all_to_all | solution.py:78
  153.6 0.7 reduce.5
  154.4 0.7 reduce.7
  155.1 14.8 %all-to-all-done = f32[8,1,32768]{2,1,0:T(1,128)S(1)} async-done(((f32[8,1,32768]{2,1,0:T(1,128)}), f32[8,1,32768]{2,1,0:T(1,128)S(1)}, u32[]{:S(2)}, u32[]{:S(2)}) %all-to-all-start) | async-done | bytes 1048608 | tf_op jit(solution)/shard_map/all_to_all | solution.py:78
  169.9 3.1 %reduce.3 = f32[8,32768]{1,0:T(8,128)S(1)} reduce(f32[8,1,32768]{2,1,0:T(1,128)S(1)} %all-to-all-done, f32[]{:T(128)} %broadcast.37), dimensions={1}, to_apply=%all_to_all.37.reduce_sub_computation | reduce | bytes 2097156 | tf_op jit(solution)/shard_map/all_to_all | solution.py:78
  173.0 2.6 %reshape.70 = f32[4096,1,64]{2,1,0:T(1,128)S(1)} reshape(f32[8,32768]{1,0:T(8,128)S(1)} %reduce.3) | data formatting | bytes 2097152
  176.0 4.0 %fusion.24 = f32[64,4096]{1,0:T(8,128)} fusion(bf16[64,512]{0,1:T(8,128)(2,1)S(1)} %fusion.21, bf16[512,4096]{1,0:T(8,128)(2,1)} %all-gather.5.cloned.1.call-done), kind=kOutput, calls=%fused_computation.38 | convolution fusion | flops 268435456 | bytes 5308416 | tf_op jit(solution)/shard_map/dot_general | solution.py:92
  180.0 62.7 %reduce-scatter.2.cloned.1.call-done = f32[64,512]{1,0:T(8,128)} async-done(((f32[64,4096]{1,0:T(8,128)}), f32[64,512]{1,0:T(8,128)}) %reduce-scatter.2.cloned.1.call-update) | async-done | bytes 131088 | tf_op jit(solution)/shard_map/reduce_scatter | solution.py:97
  242.7 1.5 convert_element_type.24
  (29 shorter events, 1.4 us)
Async XLA Ops:
  6.5 43.0 %all-gather.3.cloned.1.call-start = ((), (), s32[]{:S(2)}) async-start(), calls=%async_computation.4 | async-start | bytes 5242880 | tf_op jit(solution)/shard_map/all_gather | solution.py:24
  7.3 168.7 %all-gather.5.cloned.1.call-start = ((), (), s32[]{:S(2)}) async-start(), calls=%async_computation.5 | async-start | bytes 5242880 | tf_op jit(solution)/shard_map/all_gather | solution.py:94
  9.6 6.6 %copy-start.1 = (bf16[64,512]{1,0:T(8,128)(2,1)S(1)}, bf16[64,512]{1,0:T(8,128)(2,1)}, u32[]{:S(2)}) copy-start(bf16[64,512]{1,0:T(8,128)(2,1)} %param.9) | copy-start | bytes 196612
  9.6 40.0 %copy-start.2 = (f32[4096]{0:T(1024)S(1)}, f32[4096]{0:T(1024)}, u32[]{:S(2)}) copy-start(f32[4096]{0:T(1024)} %param.10) | copy-start | bytes 49156
  89.6 3.2 %copy-start = (f32[64,64,512]{2,1,0:T(8,128)}, f32[64,64,512]{2,1,0:T(8,128)S(1)}, u32[]{:S(2)}) copy-start(f32[64,64,512]{2,1,0:T(8,128)S(1)} %get-tuple-element.28) | copy-start | bytes 25165828
  94.7 13.5 %all-to-all-start.2 = ((f32[8,1,512]{2,1,0:T(1,128)}), f32[8,1,512]{2,1,0:T(1,128)S(1)}, u32[]{:S(2)}, u32[]{:S(2)}) async-start(f32[8,1,512]{2,1,0:T(1,128)} %reshape.73), calls=%async_computation.2 | async-start | bytes 32768 | tf_op jit(solution)/shard_map/all_to_all | solution.py:77
  100.1 6.5 %copy-start.3 = (f32[1,4,64]{2,1,0:T(4,128)S(1)}, f32[1,4,64]{2,1,0:T(4,128)}, u32[]{:S(2)}) copy-start(f32[1,4,64]{2,1,0:T(4,128)} %param.15) | copy-start | bytes 3076
  108.2 39.1 %all-to-all-start.1 = ((f32[8,1,512]{2,1,0:T(1,128)}), f32[8,1,512]{2,1,0:T(1,128)S(1)}, u32[]{:S(2)}, u32[]{:S(2)}) async-start(f32[8,1,512]{2,1,0:T(1,128)} %reshape.71), calls=%async_computation.1 | async-start | bytes 32768 | tf_op jit(solution)/shard_map/all_to_all | solution.py:76
  147.3 22.6 %all-to-all-start = ((f32[8,1,32768]{2,1,0:T(1,128)}), f32[8,1,32768]{2,1,0:T(1,128)S(1)}, u32[]{:S(2)}, u32[]{:S(2)}) async-start(f32[8,1,32768]{2,1,0:T(1,128)} %reshape.69), calls=%async_computation | async-start | bytes 2097152 | tf_op jit(solution)/shard_map/all_to_all | solution.py:78
  153.3 89.4 %reduce-scatter.2.cloned.1.call-start = ((), (), s32[]{:S(2)}) async-start(), calls=%async_computation.6 | async-start | bytes 1179648 | tf_op jit(solution)/shard_map/reduce_scatter | solution.py:97
Sparse Core Ops, SparseCore 0:
  8.9 37.1 all-gather.2
  47.7 34.4 all-gather.4
  180.2 62.5 reduce-scatter.1
where the time goes:
time: 252 us; the launch traced here: 251 us
  waiting for transfers between devices  78.9 us (31%)
  blocking collectives  64.8 us (26%)
  other arithmetic  30 us (12%)
  local copies, waits for them, and re-layouts  25.7 us (10%)
  matrix products  19.8 us (8%)
  starting transfers between devices  17.6 us (7%)
  between operations  14 us (6%)
    reduce_scatter x1, waiting for transfers between devices, per_device(): lax.psum_scatter(partial_terms, 'seg', scatter_dimension=1, tiled=True)  62.7 us
    all_gather x1, blocking collectives, per_device(): gathered = lax.all_gather(decoder_rows, 'seg', axis=1, tiled=True)  33.2 us
    all_gather x1, blocking collectives, per_device(): queries = lax.all_gather(query_own, 'seg', axis=1, tiled=True)  31.6 us
    unnamed x19, local copies, waits for them, and re-layouts  21.5 us
    unnamed x3, other arithmetic  20.7 us
    all_to_all x1, waiting for transfers between devices, per_device(): lax.all_to_all(outputs[None], 'seg', split_axis=2, concat_axis=0, tiled=T...  14.8 us
    dot_general x1, matrix products, one_doc(): jnp.einsum('qhk,khd->qhd', scaled, split_values, preferred_element_type=j...  8.51 us
    all_to_all x1, starting transfers between devices, per_device(): lax.all_to_all(outputs[None], 'seg', split_axis=2, concat_axis=0, tiled=T...  6 us
  transfers between devices with their start and end apart: 6, of which 2 were waited for; matrix products, arithmetic and copies ran while one was open for 28% of the time, Pallas kernels for 0%

commit v1 on v0

--- a/solution.py
+++ b/solution.py
@@ -75,7 +75,12 @@
     received = (
         lax.all_to_all(peaks[None], "seg", split_axis=2, concat_axis=0, tiled=True),
         lax.all_to_all(totals[None], "seg", split_axis=2, concat_axis=0, tiled=True),
-        lax.all_to_all(outputs[None], "seg", split_axis=2, concat_axis=0, tiled=True),
+        jnp.concatenate(
+            lax.all_to_all(
+                jnp.stack(jnp.split(outputs[None], lax.axis_size("seg"), axis=2)), "seg", 0, 0
+            ),
+            axis=0,
+        ),
     )
     peak_all, total_all, out_all = received
     largest = jnp.max(peak_all, axis=0)

time: 252 us -> 233 us (0.925)
  other arithmetic: 30 us -> 10.7 us
  waiting for transfers between devices: 78.9 us -> 84.4 us
  matrix products: 19.8 us -> 15.5 us
    unnamed x3 -> x2, other arithmetic: 20.7 us -> 1.39 us
    all_to_all x1, waiting for transfers between devices: 0.01 us -> 6.02 us  [per_device(): lax.all_to_all(peaks[None], 'seg', split_axis=2, concat_axis=0, tiled=True)]
    dot_general x1, matrix products: 8.51 us -> 3.89 us  [one_doc(): jnp.einsum('qhk,khd->qhd', scaled, split_values, preferred_element_type=j...]
    all_to_all x1 -> x0, other arithmetic: 3.1 us -> none  [per_device(): lax.all_to_all(outputs[None], 'seg', split_axis=2, concat_axis=0, tiled=T...]
    transpose x0 -> x1, local copies, waits for them, and re-layouts: none -> 2.81 us  [one_doc(): jnp.einsum('qhk,khd->qhd', scaled, split_values, preferred_element_type=j...]
    unnamed x19 -> x24, local copies, waits for them, and re-layouts: 21.5 us -> 19.8 us
  transfers between devices with their start and end apart: 6 -> 6, of which waited for: 2 -> 4; matrix products, arithmetic and copies ran while one was open for 28% -> 21% of each run, Pallas kernels for 0% -> 0%
where the time goes in v1:
time: 233 us; the launch traced here: 232 us
  waiting for transfers between devices  84.4 us (36%)
  blocking collectives  64.4 us (28%)
  local copies, waits for them, and re-layouts  27.7 us (12%)
  starting transfers between devices  15.5 us (7%)
  matrix products  15.5 us (7%)
  between operations  14 us (6%)
  other arithmetic  10.7 us (5%)
    reduce_scatter x1, waiting for transfers between devices, per_device(): lax.psum_scatter(partial_terms, 'seg', scatter_dimension=1, tiled=True)  63.1 us
    all_gather x1, blocking collectives, per_device(): gathered = lax.all_gather(decoder_rows, 'seg', axis=1, tiled=True)  33.2 us
    all_gather x1, blocking collectives, per_device(): queries = lax.all_gather(query_own, 'seg', axis=1, tiled=True)  31.2 us
    unnamed x24, local copies, waits for them, and re-layouts  19.8 us
    all_to_all x1, waiting for transfers between devices, per_device(): lax.all_to_all(jnp.stack(jnp.split(outputs[None], lax.axis_size('seg'), a...  13.2 us
    all_to_all x1, waiting for transfers between devices, per_device(): lax.all_to_all(peaks[None], 'seg', split_axis=2, concat_axis=0, tiled=True)  6.02 us
    all_to_all x1, starting transfers between devices, per_device(): lax.all_to_all(totals[None], 'seg', split_axis=2, concat_axis=0, tiled=True)  5.74 us
    all_to_all x1, starting transfers between devices, per_device(): lax.all_to_all(peaks[None], 'seg', split_axis=2, concat_axis=0, tiled=True)  5.4 us
  transfers between devices with their start and end apart: 6, of which 4 were waited for; matrix products, arithmetic and copies ran while one was open for 21% of the time, Pallas kernels for 0%

profile of v1, /device:TPU:0, one launch (start us, length us, event | category | flops | bytes accessed | tf_op | source)
XLA Modules:
  0.0 232.2 jit_solution(5794483273872354023)
XLA Ops:
  6.5 0.7 all-gather.3.cloned.1.call-update
  7.3 0.7 all-gather.5.cloned.1.call-update
  8.0 33.2 %all_gather.12 = bf16[64,4096]{1,0:T(8,128)(2,1)S(1)} all-gather(bf16[64,512]{1,0:T(8,128)(2,1)} %param.9), channel_id=1, replica_groups=mesh['seg'=8,'rep'=4] {'seg'}, dimensions={1}, use_global_device_ids=true | all-gather | bytes 589824 | tf_op jit(solution)/shard_map/all_gather | solution.py:18
  41.5 0.8 copy.27
  43.1 6.6 %copy.25 = bf16[1,512,4096]{1,2,0:T(8,128)(2,1)} copy(bf16[1,512,4096]{2,1,0:T(8,128)(2,1)} %param.12) | data formatting | bytes 8388608 | tf_op args[3]
  49.6 6.5 %copy.30 = bf16[1,512,4096]{1,2,0:T(8,128)(2,1)} copy(bf16[1,512,4096]{2,1,0:T(8,128)(2,1)} %param.14) | data formatting | bytes 8388608 | tf_op args[5]
  56.5 3.3 %convolution_convert_fusion = bf16[64,512]{1,0:T(8,128)(2,1)S(1)} fusion(bf16[4096,512]{1,0:T(8,128)(2,1)} %all-gather.3.cloned.1.call-done, bf16[64,4096]{1,0:T(8,128)(2,1)S(1)} %all_gather.12, f32[4096]{0:T(1024)S(1)} %copy-done.2, f32[64]{0:T(128)S(1)} %add_rsqrt_fusion), kind=kOutput, calls=%fused_computation.18 | convolution fusion | flops 269516800 | bytes 4800768 | tf_op jit(solution)/shard_map/dot_general | solution.py:22
  59.8 31.2 %all_gather.14 = bf16[64,4096]{1,0:T(8,128)(2,1)S(1)} all-gather(bf16[64,512]{1,0:T(8,128)(2,1)S(1)} %convolution_convert_fusion), channel_id=1, replica_groups=mesh['seg'=8,'rep'=4] {'seg'}, dimensions={1}, use_global_device_ids=true | all-gather | bytes 589824 | tf_op jit(solution)/shard_map/all_gather | solution.py:27
  91.0 1.1 reshape.62
  92.1 4.3 %bitcast_reduce_fusion = (f32[64,64]{0,1:T(8,128)S(1)}, f32[64,64,512]{2,1,0:T(8,128)S(1)}) fusion(f32[64,512]{1,0:T(8,128)S(1)} %bitcast.96, pred[512]{0:T(512)(128)(4,1)S(1)} %add_compare_fusion, bf16[512,64,64]{0,2,1:T(8,128)(2,1)} %bitcast.94, bf16[64,64,64]{2,1,0:T(8,128)(2,1)S(1)} %reshape.62), kind=kOutput, calls=%fused_computation.1 | convolution fusion | flops 274722816 | bytes 13255168 | tf_op jit(solution)/shard_map/while/body/eval_jaxpr/qhd,khd->qhk/dot_general | solution.py:49
  96.4 3.9 %fusion.11 = f32[64,64,64]{2,0,1:T(8,128)} fusion(bf16[512,64,64]{0,2,1:T(8,128)(2,1)S(1)} %bitcast.95, f32[64,64,512]{2,1,0:T(8,128)S(1)} %get-tuple-element.28, f32[64,512]{1,0:T(8,128)S(1)} %bitcast.105, f32[64,64]{0,1:T(8,128)S(1)} %get-tuple-element.27, f32[64,512]{1,0:T(8,128)S(1)} %bitcast.97, pred[512]{0:T(512)(128)(4,1)S(1)} %add_compare_fusion), kind=kOutput, calls=%fused_computation.15 | convolution fusion | flops 281018368 | bytes 13910528 | tf_op jit(solution)/shard_map/while/body/eval_jaxpr/qhk,khd->qhd/dot_general | solution.py:61
  100.3 2.8 %copy.31 = f32[64,64,64]{2,1,0:T(8,128)S(1)} copy(f32[64,64,64]{2,0,1:T(8,128)} %fusion.11) | data formatting | bytes 2097152 | tf_op jit(solution)/shard_map/while/body/eval_jaxpr/qhk,khd->qhd/transpose | solution.py:61
  103.8 4.8 %fusion.2 = f32[64,64]{0,1:T(8,128)S(1)} fusion(f32[64,64,512]{2,1,0:T(8,128)} %copy-done, f32[64,64]{0,1:T(8,128)S(1)} %get-tuple-element.27, f32[64,512]{1,0:T(8,128)S(1)} %bitcast.98, pred[512]{0:T(512)(128)(4,1)S(1)} %add_compare_fusion), kind=kLoop, calls=%fused_computation.6 | loop fusion | flops 10481664 | bytes 8552960 | tf_op jit(solution)/shard_map/while/body/eval_jaxpr/reduce_sum | solution.py:59
  109.1 0.7 reduce.2
  109.8 0.7 reshape.69
  110.5 5.7 %all-to-all-start.2 = ((f32[8,1,512]{2,1,0:T(1,128)}), f32[8,1,512]{2,1,0:T(1,128)S(1)}, u32[]{:S(2)}, u32[]{:S(2)}) async-start(f32[8,1,512]{2,1,0:T(1,128)} %reshape.69), calls=%async_computation.2 | async-start | bytes 32768 | tf_op jit(solution)/shard_map/all_to_all | solution.py:77
  116.9 0.7 fusion.26
  118.2 0.7 fusion.24
  119.5 0.7 fusion.22
  120.8 0.7 reduce.4
  121.5 0.7 reshape.67
  122.8 5.4 %all-to-all-start.1 = ((f32[8,1,512]{2,1,0:T(1,128)}), f32[8,1,512]{2,1,0:T(1,128)S(1)}, u32[]{:S(2)}, u32[]{:S(2)}) async-start(f32[8,1,512]{2,1,0:T(1,128)} %reshape.67), calls=%async_computation.1 | async-start | bytes 32768 | tf_op jit(solution)/shard_map/all_to_all | solution.py:76
  128.2 0.7 fusion.20
  128.9 6.0 %all-to-all-done.1 = f32[8,1,512]{2,1,0:T(1,128)S(1)} async-done(((f32[8,1,512]{2,1,0:T(1,128)}), f32[8,1,512]{2,1,0:T(1,128)S(1)}, u32[]{:S(2)}, u32[]{:S(2)}) %all-to-all-start.1) | async-done | bytes 16416 | tf_op jit(solution)/shard_map/all_to_all | solution.py:76
  134.9 4.2 %all-to-all-start = ((f32[8,1,64,512]{3,2,1,0:T(8,128)}), f32[8,1,64,512]{3,2,1,0:T(8,128)}, u32[]{:S(2)}, u32[]{:S(2)}) async-start(f32[8,1,64,512]{3,2,1,0:T(8,128)} %fusion.20), calls=%async_computation | async-start | bytes 2097152 | tf_op jit(solution)/shard_map/all_to_all | solution.py:79
  139.2 0.7 reduce.3
  139.9 0.7 reduce.5
  142.3 13.2 %all-to-all-done = f32[8,1,64,512]{3,2,1,0:T(8,128)} async-done(((f32[8,1,64,512]{3,2,1,0:T(8,128)}), f32[8,1,64,512]{3,2,1,0:T(8,128)}, u32[]{:S(2)}, u32[]{:S(2)}) %all-to-all-start) | async-done | bytes 1048608 | tf_op jit(solution)/shard_map/all_to_all | solution.py:79
  155.5 1.4 multiply_reduce_fusion
  157.0 4.0 %fusion.28 = f32[64,4096]{1,0:T(8,128)} fusion(bf16[512,4096]{1,0:T(8,128)(2,1)} %all-gather.5.cloned.1.call-done, f32[64,512]{1,0:T(8,128)S(1)} %multiply_reduce_fusion, f32[64,512]{1,0:T(8,128)S(1)} %div.20), kind=kOutput, calls=%fused_computation.46 | convolution fusion | flops 268500992 | bytes 5505024 | tf_op jit(solution)/shard_map/dot_general | solution.py:97
  161.0 63.1 %reduce-scatter.2.cloned.1.call-done = f32[64,512]{1,0:T(8,128)} async-done(((f32[64,4096]{1,0:T(8,128)}), f32[64,512]{1,0:T(8,128)}) %reduce-scatter.2.cloned.1.call-update) | async-done | bytes 131088 | tf_op jit(solution)/shard_map/reduce_scatter | solution.py:102
  224.2 1.5 convert_element_type.24
  (39 shorter events, 6.9 us)
Async XLA Ops:
  6.5 49.9 %all-gather.3.cloned.1.call-start = ((), (), s32[]{:S(2)}) async-start(), calls=%async_computation.4 | async-start | bytes 5242880 | tf_op jit(solution)/shard_map/all_gather | solution.py:24
  7.3 149.7 %all-gather.5.cloned.1.call-start = ((), (), s32[]{:S(2)}) async-start(), calls=%async_computation.5 | async-start | bytes 5242880 | tf_op jit(solution)/shard_map/all_gather | solution.py:99
  43.1 13.1 %copy-start.3 = (f32[1,4,64]{2,1,0:T(4,128)S(1)}, f32[1,4,64]{2,1,0:T(4,128)}, u32[]{:S(2)}) copy-start(f32[1,4,64]{2,1,0:T(4,128)} %param.15) | copy-start | bytes 3076
  43.1 13.4 %copy-start.2 = (f32[4096]{0:T(1024)S(1)}, f32[4096]{0:T(1024)}, u32[]{:S(2)}) copy-start(f32[4096]{0:T(1024)} %param.10) | copy-start | bytes 49156
  92.1 4.4 %copy-start.1 = (bf16[1,512,4096]{1,2,0:T(8,128)(2,1)S(1)}, bf16[1,512,4096]{1,2,0:T(8,128)(2,1)}, u32[]{:S(2)}) copy-start(bf16[1,512,4096]{1,2,0:T(8,128)(2,1)} %copy.30) | copy-start | bytes 12582916
  96.4 3.9 %copy-start = (f32[64,64,512]{2,1,0:T(8,128)}, f32[64,64,512]{2,1,0:T(8,128)S(1)}, u32[]{:S(2)}) copy-start(f32[64,64,512]{2,1,0:T(8,128)S(1)} %get-tuple-element.28) | copy-start | bytes 25165828
  110.5 12.3 %all-to-all-start.2 = ((f32[8,1,512]{2,1,0:T(1,128)}), f32[8,1,512]{2,1,0:T(1,128)S(1)}, u32[]{:S(2)}, u32[]{:S(2)}) async-start(f32[8,1,512]{2,1,0:T(1,128)} %reshape.69), calls=%async_computation.2 | async-start | bytes 32768 | tf_op jit(solution)/shard_map/all_to_all | solution.py:77
  122.8 12.1 %all-to-all-start.1 = ((f32[8,1,512]{2,1,0:T(1,128)}), f32[8,1,512]{2,1,0:T(1,128)S(1)}, u32[]{:S(2)}, u32[]{:S(2)}) async-start(f32[8,1,512]{2,1,0:T(1,128)} %reshape.67), calls=%async_computation.1 | async-start | bytes 32768 | tf_op jit(solution)/shard_map/all_to_all | solution.py:76
  134.9 20.6 %all-to-all-start = ((f32[8,1,64,512]{3,2,1,0:T(8,128)}), f32[8,1,64,512]{3,2,1,0:T(8,128)}, u32[]{:S(2)}, u32[]{:S(2)}) async-start(f32[8,1,64,512]{3,2,1,0:T(8,128)} %fusion.20), calls=%async_computation | async-start | bytes 2097152 | tf_op jit(solution)/shard_map/all_to_all | solution.py:79
  139.1 85.0 %reduce-scatter.2.cloned.1.call-start = ((), (), s32[]{:S(2)}) async-start(), calls=%async_computation.6 | async-start | bytes 1179648 | tf_op jit(solution)/shard_map/reduce_scatter | solution.py:102
Sparse Core Ops, SparseCore 0:
  8.9 37.1 all-gather.2
  47.7 34.4 all-gather.4
  161.1 62.9 reduce-scatter.1
